TPU v7x, 32 devices: a whole 2x2x4 slice. The times are simulated.
32 devices in a mesh: dp: 2 (over x), cluster: 16 (over z, y, core).
Axes of the slice: x: 2, y: 2, z: 4, core: 2. Of those that a mesh axis runs over, the one named last changes fastest.
Arguments:
- queries: bfloat16 [4096, 768], P(('dp', 'cluster')), may hold values from -6 to 6
- shortlist: int32 [4096, 8], P(('dp', 'cluster')), may hold values from 0 to 15, all different within a row; in each aligned block of 128 rows (0 to 127, 128 to 255, ...) at most 128 rows name the same one
- positives: int32 [4096, 8], P(('dp', 'cluster')), may hold values from 0 to 255
- weights: bfloat16 [16, 256, 768], P('cluster'), may hold values from -0.21875 to 0.21875
- first_moment: float32 [16, 256, 768], P('cluster'), may hold values from -24 to 24
- second_moment: float32 [16, 256, 768], P('cluster'), may hold values from 0.5 to 50
Outputs:
- new_weights: bfloat16 [16, 256, 768], P('cluster')
- new_first: float32 [16, 256, 768], P('cluster')
- new_second: float32 [16, 256, 768], P('cluster')
- query_grad: bfloat16 [4096, 768], P(('dp', 'cluster'))
Inputs may be any that keep to these rules, and one draw needn't show every extreme that they name: `shortlist`: each row names 8 different clusters. In the rows of one device no cluster is named by more than 128 rows, a bound that some block reaches of them.
All inputs are finite; a program needn't handle non-finite values.
Results may differ from a plain program's by a relative error of at most 0.0085.
Values may be sent and summed in bfloat16 or wider, within the bound.
No kernel may reach another device: no remote copies, remote signals or barrier semaphores. Data moves between devices by JAX's collectives and lax.ppermute only.
A program may use at most 64 MiB of HBM per device.

v0:
```python
import jax
import jax.numpy as jnp
from jax import lax
from jax.sharding import PartitionSpec as P

beta_one = 0.9
beta_two = 0.999
learn_rate = 0.01
adam_eps = 1e-08
adam_step = 10.0


def adam_update(cluster_weights, first_moment, second_moment, gradient):
    first_new = beta_one * first_moment + (1.0 - beta_one) * gradient
    second_new = beta_two * second_moment + (1.0 - beta_two) * gradient * gradient
    first_hat = first_new / (1.0 - beta_one**adam_step)
    second_hat = second_new / (1.0 - beta_two**adam_step)
    stepped = cluster_weights.astype(jnp.float32) - learn_rate * first_hat / (
        jnp.sqrt(second_hat) + adam_eps
    )
    return (stepped.astype(jnp.bfloat16), first_new, second_new)


def owner_work(arrived_rows, arrived_labels, cluster_rows):
    label_ids = jnp.arange(cluster_rows.shape[0], dtype=jnp.int32)
    scores = lax.dot_general(
        arrived_rows, cluster_rows, (((1,), (1,)), ((), ())), preferred_element_type=jnp.float32
    )
    target = (arrived_labels[:, None] == label_ids[None, :]).astype(jnp.float32)
    coefficient = (jax.nn.sigmoid(scores) - target).astype(jnp.bfloat16)
    gradient = lax.dot_general(
        coefficient, arrived_rows, (((0,), (0,)), ((), ())), preferred_element_type=jnp.float32
    )
    visit_grad = jnp.dot(coefficient, cluster_rows, preferred_element_type=jnp.float32).astype(
        jnp.bfloat16
    )
    return (gradient, visit_grad)


def on_device(queries, shortlist, positives, weights, first_moment, second_moment):
    owners = lax.axis_size("cluster")
    rows_dev, fanout = shortlist.shape
    feature_dim = queries.shape[1]
    capacity = min(rows_dev, 2 * rows_dev * fanout // owners)
    visits = shortlist.reshape(-1)
    labels = positives.reshape(-1)
    onehot = (visits[:, None] == jnp.arange(owners, dtype=jnp.int32)[None, :]).astype(jnp.int32)
    visit_rank = jnp.sum((jnp.cumsum(onehot, axis=0) - onehot) * onehot, axis=1)
    slot_index = visits * capacity + visit_rank
    slot_visit = (
        jnp.full((owners * capacity,), -1, jnp.int32)
        .at[slot_index]
        .set(jnp.arange(visits.shape[0], dtype=jnp.int32))
    )
    filled = slot_visit >= 0
    clamped = jnp.maximum(slot_visit, 0)
    send_rows = jnp.where(filled[:, None], queries[clamped // fanout], jnp.zeros((), queries.dtype))
    send_labels = jnp.where(filled, labels[clamped], -1)
    cluster_rows = weights[0]
    arrived_rows, arrived_labels = (
        lax.all_to_all(
            send_rows.reshape(owners, capacity, feature_dim),
            "cluster",
            split_axis=0,
            concat_axis=0,
            tiled=True,
        ),
        lax.all_to_all(
            send_labels.reshape(owners, capacity),
            "cluster",
            split_axis=0,
            concat_axis=0,
            tiled=True,
        ),
    )
    gradient, visit_grad = owner_work(
        arrived_rows.reshape(-1, feature_dim), arrived_labels.reshape(-1), cluster_rows
    )
    returned = lax.all_to_all(
        visit_grad.reshape(owners, capacity, feature_dim),
        "cluster",
        split_axis=0,
        concat_axis=0,
        tiled=True,
    )
    per_visit = returned.reshape(-1, feature_dim)[slot_index].astype(jnp.float32)
    query_grad = jnp.sum(per_visit.reshape(rows_dev, fanout, feature_dim), axis=1).astype(
        jnp.bfloat16
    )
    summed = lax.psum(gradient.astype(jnp.bfloat16), "dp").astype(jnp.float32)
    new_weights, new_first, new_second = adam_update(
        cluster_rows, first_moment[0], second_moment[0], summed
    )
    return (new_weights[None], new_first[None], new_second[None], query_grad)


def solution(mesh):
    in_specs = (
        P(("dp", "cluster"), None),
        P(("dp", "cluster"), None),
        P(("dp", "cluster"), None),
        P("cluster", None, None),
        P("cluster", None, None),
        P("cluster", None, None),
    )
    out_specs = (
        P("cluster", None, None),
        P("cluster", None, None),
        P("cluster", None, None),
        P(("dp", "cluster"), None),
    )
    return jax.shard_map(
        on_device, mesh=mesh, in_specs=in_specs, out_specs=out_specs, check_vma=False
    )
```

profile of v0, /device:TPU:13, one launch (start us, length us, event | category | flops | bytes accessed | tf_op | source)
XLA Modules:
  0.0 218.1 jit_solution(6871849412178040356)
XLA Ops:
  7.2 0.0 copy-start
  7.2 0.7 broadcast_multiply_fusion
  7.9 0.8 copy.13
  8.7 0.1 eq.44
  8.8 0.1 eq.40
  8.9 0.1 copy.12
  9.0 0.1 mul.63
  9.1 4.5 %reduce-window.6 = s32[16,8,128]{2,1,0:T(8,128)S(1)} reduce-window(s32[16,8,128]{2,1,0:T(8,128)S(1)} %fusion.15, s32[]{:T(128)} %constant.23.clone.1), window={size=1x1x128 pad=0_0x0_0x127_0}, to_apply=%region_0.0 | reduce-window | flops 2080768 | bytes 131076 | tf_op jit(solution)/shard_map/reduce-window
  13.6 0.1 slice.14
  13.7 0.1 copy.15
  13.9 0.1 copy.16
  13.9 0.1 broadcast_add_fusion
  14.1 4.3 %scatter_custom_fusion = s32[2048]{0:T(1024)S(1)} fusion(s32[1024]{0:T(1024)S(1)} %bitcast.72, s32[1024]{0:T(1024)S(1)} %iota.15, s32[]{:T(128)} %constant.20.clone.1), kind=kCustom, calls=%fused_computation.43 | custom fusion | bytes 8196 | tf_op jit(solution)/shard_map/scatter | solution.py:53
  18.4 0.8 copy.17
  19.2 0.1 reshape.88
  19.3 8.6 %gather_fusion.1 = s32[2048]{0:T(1024)S(1)} fusion(s32[1024]{0:T(1024)S(1)} %reshape.88, s32[2048]{0:T(1024)S(1)} %maximum_clamp_fusion), kind=kCustom, calls=%fused_computation.1 | custom fusion | bytes 24576 | tf_op jit(solution)/shard_map/gather | solution.py:58
  27.9 0.6 broadcast_select_fusion.1
  28.5 6.5 %all-to-all-start.1 = ((s32[16,1,128]{2,1,0:T(1,128)}), s32[16,1,128]{2,1,0:T(1,128)S(1)}, u32[]{:S(2)}, u32[]{:S(2)}) async-start(s32[16,1,128]{2,1,0:T(1,128)} %bitcast.9), calls=%async_computation.1 | async-start | bytes 16384 | tf_op jit(solution)/shard_map/all_to_all | solution.py:68
  35.0 0.0 copy-done
  35.0 9.4 %gather_fusion = bf16[2048,768]{1,0:T(8,128)(2,1)} fusion(bf16[128,768]{1,0:T(8,128)(2,1)S(1)} %copy-done, s32[2048]{0:T(1024)S(1)} %get-tuple-element.9), kind=kCustom, calls=%fused_computation | custom fusion | bytes 6299648 | tf_op jit(solution)/shard_map/gather | solution.py:57
  44.4 2.1 broadcast_select_fusion
  46.5 0.0 all-to-all-done.1
  46.5 0.0 copy-start.3
  46.5 75.7 %all_to_all.19 = bf16[16,128,768]{2,1,0:T(8,128)(2,1)S(1)} all-to-all(bf16[16,128,768]{2,1,0:T(8,128)(2,1)S(1)} %broadcast_select_fusion), channel_id=1, replica_groups=mesh['dp'=2,'cluster'=16] {'cluster'}, dimensions={0} | all-to-all | bytes 6291456 | tf_op jit(solution)/shard_map/all_to_all | solution.py:61
  122.2 0.0 copy-start.2
  122.2 1.7 copy-done.2
  123.9 0.0 copy-done.3
  123.9 1.3 fusion.4
  125.3 0.0 copy-start.1
  125.3 2.7 %convolution_convert_fusion = bf16[2048,768]{1,0:T(8,128)(2,1)} fusion(bf16[2048,256]{1,0:T(8,128)(2,1)S(1)} %fusion.4, bf16[1,256,768]{2,1,0:T(8,128)(2,1)S(1)} %copy-done.3), kind=kOutput, calls=%fused_computation.4 | convolution fusion | flops 806879232 | bytes 4587520 | tf_op jit(solution)/shard_map/dot_general | solution.py:34
  127.9 0.0 copy-done.1
  127.9 5.1 %all-to-all-start.2 = ((bf16[16,128,768]{2,1,0:T(8,128)(2,1)}), bf16[16,128,768]{2,1,0:T(8,128)(2,1)S(1)}, u32[]{:S(2)}, u32[]{:S(2)}) async-start(bf16[16,128,768]{2,1,0:T(8,128)(2,1)} %bitcast.65), calls=%async_computation.2 | async-start | bytes 6291456 | tf_op jit(solution)/shard_map/all_to_all | solution.py:79
  133.0 0.0 all-reduce.2.cloned.1.call-start
  133.1 4.0 %convolution_convert_fusion.1 = bf16[256,768]{1,0:T(8,128)(2,1)} fusion(bf16[2048,256]{1,0:T(8,128)(2,1)} %copy-done.1, bf16[2048,768]{1,0:T(8,128)(2,1)} %bitcast.68), kind=kOutput, calls=%fused_computation.14 | convolution fusion | flops 805502976 | bytes 4587520 | tf_op jit(solution)/shard_map/dot_general | solution.py:31
  137.1 0.0 all-reduce.2.cloned.1.call-update
  137.1 26.4 %all-reduce.2.cloned.1.call-done = bf16[256,768]{1,0:T(8,128)(2,1)} async-done(((bf16[256,768]{1,0:T(8,128)(2,1)}), bf16[256,768]{1,0:T(8,128)(2,1)}) %all-reduce.2.cloned.1.call-update) | async-done | bytes 393232 | tf_op jit(solution)/shard_map/psum | solution.py:90
  163.5 3.4 %fusion.8 = (f32[1,256,768]{2,1,0:T(8,128)}, bf16[1,256,768]{2,1,0:T(8,128)(2,1)}, f32[1,256,768]{2,1,0:T(8,128)}) fusion(bf16[256,768]{1,0:T(8,128)(2,1)} %all-reduce.2.cloned.1.call-done, f32[1,256,768]{2,1,0:T(8,128)} %param.11, f32[1,256,768]{2,1,0:T(8,128)} %param.10, bf16[1,256,768]{2,1,0:T(8,128)(2,1)} %param.9), kind=kLoop, calls=%fused_computation.21 | loop fusion | flops 2949120 | bytes 4325376 | tf_op jit(solution)/shard_map/broadcast_in_dim | solution.py:94
  166.9 36.0 %all-to-all-done.2 = bf16[16,128,768]{2,1,0:T(8,128)(2,1)S(1)} async-done(((bf16[16,128,768]{2,1,0:T(8,128)(2,1)}), bf16[16,128,768]{2,1,0:T(8,128)(2,1)S(1)}, u32[]{:S(2)}, u32[]{:S(2)}) %all-to-all-start.2) | async-done | bytes 3145760 | tf_op jit(solution)/shard_map/all_to_all | solution.py:79
  202.9 5.2 %gather_fusion.2 = bf16[1024,768]{1,0:T(8,128)(2,1)} fusion(bf16[2048,768]{1,0:T(8,128)(2,1)S(1)} %bitcast.64, s32[1024]{0:T(1024)S(1)} %broadcast_clamp_fusion), kind=kCustom, calls=%fused_computation.2 | custom fusion | bytes 3149824 | tf_op jit(solution)/shard_map/gather | solution.py:86
  208.1 3.1 %bitcast_reduce_fusion = bf16[128,768]{1,0:T(8,128)(2,1)} fusion(bf16[1024,768]{1,0:T(8,128)(2,1)} %gather_fusion.2), kind=kLoop, calls=%fused_computation.13 | loop fusion | flops 688128 | bytes 1769472 | tf_op jit(solution)/shard_map/reduce_sum | solution.py:87
  (8 shorter events, 0.1 us)
Async XLA Ops:
  7.2 27.9 %copy-start = (bf16[128,768]{1,0:T(8,128)(2,1)S(1)}, bf16[128,768]{1,0:T(8,128)(2,1)}, u32[]{:S(2)}) copy-start(bf16[128,768]{1,0:T(8,128)(2,1)} %param.6) | copy-start | bytes 589828
  28.5 18.0 %all-to-all-start.1 = ((s32[16,1,128]{2,1,0:T(1,128)}), s32[16,1,128]{2,1,0:T(1,128)S(1)}, u32[]{:S(2)}, u32[]{:S(2)}) async-start(s32[16,1,128]{2,1,0:T(1,128)} %bitcast.9), calls=%async_computation.1 | async-start | bytes 16384 | tf_op jit(solution)/shard_map/all_to_all | solution.py:68
  46.5 77.4 %copy-start.3 = (bf16[1,256,768]{2,1,0:T(8,128)(2,1)S(1)}, bf16[1,256,768]{2,1,0:T(8,128)(2,1)}, u32[]{:S(2)}) copy-start(bf16[1,256,768]{2,1,0:T(8,128)(2,1)} %param.9) | copy-start | bytes 1179652
  122.2 1.7 copy-start.2
  125.3 2.7 %copy-start.1 = (bf16[2048,256]{1,0:T(8,128)(2,1)}, bf16[2048,256]{1,0:T(8,128)(2,1)S(1)}, u32[]{:S(2)}) copy-start(bf16[2048,256]{1,0:T(8,128)(2,1)S(1)} %fusion.4) | copy-start | bytes 3145732
  127.9 75.0 %all-to-all-start.2 = ((bf16[16,128,768]{2,1,0:T(8,128)(2,1)}), bf16[16,128,768]{2,1,0:T(8,128)(2,1)S(1)}, u32[]{:S(2)}, u32[]{:S(2)}) async-start(bf16[16,128,768]{2,1,0:T(8,128)(2,1)} %bitcast.65), calls=%async_computation.2 | async-start | bytes 6291456 | tf_op jit(solution)/shard_map/all_to_all | solution.py:79
  133.0 30.4 %all-reduce.2.cloned.1.call-start = ((), (), s32[]{:S(2)}) async-start(), calls=%async_computation.3 | async-start | bytes 786432 | tf_op jit(solution)/shard_map/psum | solution.py:90
Sparse Core Ops, SparseCore 0:
  137.2 26.2 all-reduce.1
where the time goes:
time: 219 us; the launch traced here: 218 us
  blocking collectives  75.7 us (35%)
  waiting for transfers between devices  62.4 us (28%)
  local copies, waits for them, and re-layouts  31.5 us (14%)
  other arithmetic  14.7 us (7%)
  between operations  14.2 us (6%)
  starting transfers between devices  11.7 us (5%)
  matrix products  7.95 us (4%)
    all_to_all x1, blocking collectives, on_device(): lax.all_to_all(send_rows.reshape(owners, capacity, feature_dim), 'cluster...  75.7 us
    all_to_all x1, waiting for transfers between devices, on_device(): lax.all_to_all(visit_grad.reshape(owners, capacity, feature_dim), 'cluste...  36 us
    psum x1, waiting for transfers between devices, on_device(): summed = lax.psum(gradient.astype(jnp.bfloat16), 'dp').astype(jnp.float32)  26.4 us
    gather x1, local copies, waits for them, and re-layouts, on_device(): queries[clamped // fanout]  9.38 us
    gather x1, local copies, waits for them, and re-layouts, on_device(): send_labels = jnp.where(filled, labels[clamped], -1)  8.58 us
    all_to_all x1, starting transfers between devices, on_device(): lax.all_to_all(send_labels.reshape(owners, capacity), 'cluster', split_ax...  6.52 us
    gather x1, local copies, waits for them, and re-layouts, on_device(): returned.reshape(-1, feature_dim)[slot_index].astype(jnp.float32)  5.21 us
    all_to_all x1, starting transfers between devices, on_device(): lax.all_to_all(visit_grad.reshape(owners, capacity, feature_dim), 'cluste...  5.1 us
  transfers between devices with their start and end apart: 3, of which 2 were waited for; matrix products, arithmetic and copies ran while one was open for 9% of the time, Pallas kernels for 0%

commit v1 on v0

--- a/solution.py
+++ b/solution.py
@@ -87,7 +87,9 @@
     query_grad = jnp.sum(per_visit.reshape(rows_dev, fanout, feature_dim), axis=1).astype(
         jnp.bfloat16
     )
-    summed = lax.psum(gradient.astype(jnp.bfloat16), "dp").astype(jnp.float32)
+    summed = jnp.sum(lax.all_gather(gradient.astype(jnp.bfloat16), "dp"), axis=0).astype(
+        jnp.float32
+    )
     new_weights, new_first, new_second = adam_update(
         cluster_rows, first_moment[0], second_moment[0], summed
     )

time: 219 us -> 205 us (0.936)
  between operations: 14.2 us -> 0.77 us
  waiting for transfers between devices: 62.4 us -> 50.3 us
  blocking collectives: 75.7 us -> 86.7 us
    psum x1 -> x0, waiting for transfers between devices: 26.4 us -> none  [on_device(): summed = lax.psum(gradient.astype(jnp.bfloat16), 'dp').astype(jnp.float32)]
    all_to_all x1, waiting for transfers between devices: 36 us -> 50.3 us  [on_device(): lax.all_to_all(visit_grad.reshape(owners, capacity, feature_dim), 'cluste...]
    all_gather x0 -> x1, blocking collectives: none -> 11 us  [on_device(): lax.all_gather(gradient.astype(jnp.bfloat16), 'dp')]
    broadcast_in_dim x1 -> x0, other arithmetic: 3.42 us -> none  [on_device(): return (new_weights[None], new_first[None], new_second[None], query_grad)]
    convert_element_type x0 -> x1, other arithmetic: none -> 3.23 us  [adam_update(): return (stepped.astype(jnp.bfloat16), first_new, second_new)]
  transfers between devices with their start and end apart: 3 -> 2, of which waited for: 2 -> 1; matrix products, arithmetic and copies ran while one was open for 9% -> 10% of each run, Pallas kernels for 0% -> 0%
where the time goes in v1:
time: 205 us
  blocking collectives  86.7 us (42%)
  waiting for transfers between devices  50.3 us (25%)
  local copies, waits for them, and re-layouts  31.5 us (15%)
  other arithmetic  16.6 us (8%)
  starting transfers between devices  11.6 us (6%)
  matrix products  7.2 us (4%)
    all_to_all x1, blocking collectives, on_device(): lax.all_to_all(send_rows.reshape(owners, capacity, feature_dim), 'cluster...  75.7 us
    all_to_all x1, waiting for transfers between devices, on_device(): lax.all_to_all(visit_grad.reshape(owners, capacity, feature_dim), 'cluste...  50.3 us
    all_gather x1, blocking collectives, on_device(): lax.all_gather(gradient.astype(jnp.bfloat16), 'dp')  11 us
    gather x1, local copies, waits for them, and re-layouts, on_device(): queries[clamped // fanout]  9.38 us
    gather x1, local copies, waits for them, and re-layouts, on_device(): send_labels = jnp.where(filled, labels[clamped], -1)  8.58 us
    all_to_all x1, starting transfers between devices, on_device(): lax.all_to_all(send_labels.reshape(owners, capacity), 'cluster', split_ax...  6.52 us
    gather x1, local copies, waits for them, and re-layouts, on_device(): returned.reshape(-1, feature_dim)[slot_index].astype(jnp.float32)  5.21 us
    all_to_all x1, starting transfers between devices, on_device(): lax.all_to_all(visit_grad.reshape(owners, capacity, feature_dim), 'cluste...  5.1 us
  transfers between devices with their start and end apart: 2, of which 1 were waited for; matrix products, arithmetic and copies ran while one was open for 10% of the time, Pallas kernels for 0%

profile of v1, /device:TPU:13, one launch (start us, length us, event | category | flops | bytes accessed | tf_op | source)
XLA Modules:
  0.0 204.7 jit_solution(3301118282861082933)
XLA Ops:
  0.6 0.0 copy-start
  0.6 0.7 broadcast_multiply_fusion
  1.4 0.8 copy.13
  2.2 0.1 eq.44
  2.3 0.1 eq.40
  2.3 0.1 copy.12
  2.4 0.1 mul.85
  2.6 4.5 %reduce-window.6 = s32[16,8,128]{2,1,0:T(8,128)S(1)} reduce-window(s32[16,8,128]{2,1,0:T(8,128)S(1)} %fusion.12, s32[]{:T(128)} %constant.24.clone.1), window={size=1x1x128 pad=0_0x0_0x127_0}, to_apply=%region_0.0 | reduce-window | flops 2080768 | bytes 131076 | tf_op jit(solution)/shard_map/reduce-window
  7.1 0.1 slice.14
  7.2 0.1 copy.15
  7.3 0.1 copy.16
  7.4 0.1 broadcast_add_fusion
  7.6 4.3 %scatter_custom_fusion = s32[2048]{0:T(1024)S(1)} fusion(s32[1024]{0:T(1024)S(1)} %bitcast.55, s32[1024]{0:T(1024)S(1)} %iota.15, s32[]{:T(128)} %constant.21.clone.1), kind=kCustom, calls=%fused_computation.41 | custom fusion | bytes 8196 | tf_op jit(solution)/shard_map/scatter | solution.py:53
  11.9 0.8 copy.17
  12.7 0.1 reshape.107
  12.8 8.6 %gather_fusion.1 = s32[2048]{0:T(1024)S(1)} fusion(s32[1024]{0:T(1024)S(1)} %reshape.107, s32[2048]{0:T(1024)S(1)} %maximum_clamp_fusion), kind=kCustom, calls=%fused_computation.1 | custom fusion | bytes 24576 | tf_op jit(solution)/shard_map/gather | solution.py:58
  21.4 0.6 broadcast_select_fusion.1
  22.0 6.5 %all-to-all-start.1 = ((s32[16,1,128]{2,1,0:T(1,128)}), s32[16,1,128]{2,1,0:T(1,128)S(1)}, u32[]{:S(2)}, u32[]{:S(2)}) async-start(s32[16,1,128]{2,1,0:T(1,128)} %bitcast.8), calls=%async_computation.1 | async-start | bytes 16384 | tf_op jit(solution)/shard_map/all_to_all | solution.py:68
  28.5 0.0 copy-done
  28.5 9.4 %gather_fusion = bf16[2048,768]{1,0:T(8,128)(2,1)} fusion(bf16[128,768]{1,0:T(8,128)(2,1)S(1)} %copy-done, s32[2048]{0:T(1024)S(1)} %get-tuple-element.9), kind=kCustom, calls=%fused_computation | custom fusion | bytes 6299648 | tf_op jit(solution)/shard_map/gather | solution.py:57
  37.9 2.1 %broadcast_select_fusion = bf16[16,128,768]{2,1,0:T(8,128)(2,1)S(1)} fusion(bf16[16,128,768]{2,1,0:T(8,128)(2,1)} %bitcast.48, pred[16,128]{1,0:T(8,128)(4,1)S(1)} %bitcast.57), kind=kLoop, calls=%fused_computation.5 | loop fusion | flops 1572864 | bytes 6293504 | tf_op jit(solution)/shard_map/jit(_where)/select_n | solution.py:57
  40.0 0.0 all-to-all-done.1
  40.0 0.0 copy-start.3
  40.0 75.7 %all_to_all.19 = bf16[16,128,768]{2,1,0:T(8,128)(2,1)S(1)} all-to-all(bf16[16,128,768]{2,1,0:T(8,128)(2,1)S(1)} %broadcast_select_fusion), channel_id=1, replica_groups=mesh['dp'=2,'cluster'=16] {'cluster'}, dimensions={0} | all-to-all | bytes 6291456 | tf_op jit(solution)/shard_map/all_to_all | solution.py:61
  115.7 0.0 copy-start.2
  115.7 1.7 copy-done.2
  117.4 0.0 copy-done.3
  117.4 1.3 fusion.4
  118.7 0.0 copy-start.1
  118.7 2.7 %convolution_convert_fusion = bf16[2048,768]{1,0:T(8,128)(2,1)} fusion(bf16[2048,256]{1,0:T(8,128)(2,1)S(1)} %fusion.4, bf16[1,256,768]{2,1,0:T(8,128)(2,1)S(1)} %copy-done.3), kind=kOutput, calls=%fused_computation.4 | convolution fusion | flops 806879232 | bytes 4587520 | tf_op jit(solution)/shard_map/dot_general | solution.py:34
  121.4 0.0 copy-done.1
  121.4 5.1 %all-to-all-start.2 = ((bf16[16,128,768]{2,1,0:T(8,128)(2,1)}), bf16[16,128,768]{2,1,0:T(8,128)(2,1)S(1)}, u32[]{:S(2)}, u32[]{:S(2)}) async-start(bf16[16,128,768]{2,1,0:T(8,128)(2,1)} %bitcast.47), calls=%async_computation.2 | async-start | bytes 6291456 | tf_op jit(solution)/shard_map/all_to_all | solution.py:79
  126.5 3.2 %convolution_convert_fusion.1 = bf16[256,768]{1,0:T(8,128)(2,1)S(1)} fusion(bf16[2048,256]{1,0:T(8,128)(2,1)} %copy-done.1, bf16[2048,768]{1,0:T(8,128)(2,1)} %bitcast.50), kind=kOutput, calls=%fused_computation.14 | convolution fusion | flops 805502976 | bytes 4587520 | tf_op jit(solution)/shard_map/dot_general | solution.py:31
  129.7 11.0 %all-gather = bf16[512,768]{1,0:T(8,128)(2,1)} all-gather(bf16[256,768]{1,0:T(8,128)(2,1)S(1)} %convolution_convert_fusion.1), channel_id=2, replica_groups=mesh['dp'=2,'cluster'=16] {'dp'}, dimensions={0}, use_global_device_ids=true | all-gather | bytes 1179648 | tf_op jit(solution)/shard_map/all_gather | solution.py:90
  140.8 2.1 %reduce_sum.37 = bf16[256,768]{1,0:T(8,128)(2,1)} reduce(bf16[2,256,768]{2,1,0:T(8,128)(2,1)} %bitcast.51, bf16[]{:T(256)} %constant.52.clone.1), dimensions={0}, to_apply=%region_4.5 | reduce | flops 196608 | bytes 1179650 | tf_op jit(solution)/shard_map/reduce_sum | solution.py:90
  142.9 3.2 %subtract_convert_fusion = (bf16[1,256,768]{2,1,0:T(8,128)(2,1)}, f32[1,256,768]{2,1,0:T(8,128)}, f32[1,256,768]{2,1,0:T(8,128)}) fusion(bf16[1,256,768]{2,1,0:T(8,128)(2,1)} %param.9, bf16[256,768]{1,0:T(8,128)(2,1)} %reduce_sum.37, f32[1,256,768]{2,1,0:T(8,128)} %param.10, f32[1,256,768]{2,1,0:T(8,128)} %param.11), kind=kLoop, calls=%fused_computation.20 | loop fusion | flops 2949120 | bytes 4325376 | tf_op jit(solution)/shard_map/convert_element_type | solution.py:21
  146.1 50.3 %all-to-all-done.2 = bf16[16,128,768]{2,1,0:T(8,128)(2,1)S(1)} async-done(((bf16[16,128,768]{2,1,0:T(8,128)(2,1)}), bf16[16,128,768]{2,1,0:T(8,128)(2,1)S(1)}, u32[]{:S(2)}, u32[]{:S(2)}) %all-to-all-start.2) | async-done | bytes 3145760 | tf_op jit(solution)/shard_map/all_to_all | solution.py:79
  196.4 5.2 %gather_fusion.2 = bf16[1024,768]{1,0:T(8,128)(2,1)} fusion(bf16[2048,768]{1,0:T(8,128)(2,1)S(1)} %bitcast.46, s32[1024]{0:T(1024)S(1)} %broadcast_clamp_fusion), kind=kCustom, calls=%fused_computation.2 | custom fusion | bytes 3149824 | tf_op jit(solution)/shard_map/gather | solution.py:86
  201.6 3.1 %bitcast_reduce_fusion = bf16[128,768]{1,0:T(8,128)(2,1)} fusion(bf16[1024,768]{1,0:T(8,128)(2,1)} %gather_fusion.2), kind=kLoop, calls=%fused_computation.13 | loop fusion | flops 688128 | bytes 1769472 | tf_op jit(solution)/shard_map/reduce_sum | solution.py:87
  (8 shorter events, 0.1 us)
Async XLA Ops:
  0.6 27.9 %copy-start = (bf16[128,768]{1,0:T(8,128)(2,1)S(1)}, bf16[128,768]{1,0:T(8,128)(2,1)}, u32[]{:S(2)}) copy-start(bf16[128,768]{1,0:T(8,128)(2,1)} %param.6) | copy-start | bytes 589828
  22.0 18.0 %all-to-all-start.1 = ((s32[16,1,128]{2,1,0:T(1,128)}), s32[16,1,128]{2,1,0:T(1,128)S(1)}, u32[]{:S(2)}, u32[]{:S(2)}) async-start(s32[16,1,128]{2,1,0:T(1,128)} %bitcast.8), calls=%async_computation.1 | async-start | bytes 16384 | tf_op jit(solution)/shard_map/all_to_all | solution.py:68
  40.0 77.4 %copy-start.3 = (bf16[1,256,768]{2,1,0:T(8,128)(2,1)S(1)}, bf16[1,256,768]{2,1,0:T(8,128)(2,1)}, u32[]{:S(2)}) copy-start(bf16[1,256,768]{2,1,0:T(8,128)(2,1)} %param.9) | copy-start | bytes 1179652
  115.7 1.7 copy-start.2
  118.7 2.7 %copy-start.1 = (bf16[2048,256]{1,0:T(8,128)(2,1)}, bf16[2048,256]{1,0:T(8,128)(2,1)S(1)}, u32[]{:S(2)}) copy-start(bf16[2048,256]{1,0:T(8,128)(2,1)S(1)} %fusion.4) | copy-start | bytes 3145732
  121.4 75.0 %all-to-all-start.2 = ((bf16[16,128,768]{2,1,0:T(8,128)(2,1)}), bf16[16,128,768]{2,1,0:T(8,128)(2,1)S(1)}, u32[]{:S(2)}, u32[]{:S(2)}) async-start(bf16[16,128,768]{2,1,0:T(8,128)(2,1)} %bitcast.47), calls=%async_computation.2 | async-start | bytes 6291456 | tf_op jit(solution)/shard_map/all_to_all | solution.py:79
